TPU v7x, 128 devices: a whole 4x4x4 slice. The times are simulated.
128 devices in a mesh: sky: 32 (over y, x, core), visit: 4 (over z).
Axes of the slice: x: 4, y: 4, z: 4, core: 2. Of those that a mesh axis runs over, the one named last changes fastest.
Arguments:
- images: bfloat16 [32, 3072, 2048], P('visit', 'sky'), may hold values from -6 to 6
- inv_var: bfloat16 [32, 3072, 2048], P('visit', 'sky'), may hold values from 0.25 to 4
- row_taps: bfloat16 [11, 41], replicated, may hold values from -1 to 1
- col_taps: bfloat16 [11, 41], replicated, may hold values from -1 to 1
- coeffs: float32 [32, 11, 3], replicated, may hold values from -4 to 4
- dithers: int32 [32], replicated, may hold values from 0 to 256, as said below
- depths: int32 [32], P('sky'), may hold values from 2 to 16, as said below
Outputs:
- coadd: float32 [3072, 2048], P('sky', 'visit')
Inputs may be any that keep to these rules, and one draw needn't show every extreme that they name: `dithers`: some visit has offset 0 and some has offset 256. `depths`: some tile is covered by 16 visits.
All inputs are finite; a program needn't handle non-finite values.
Results may differ from a plain program's by a relative error of at most 0.0029.
Values may be sent and summed in bfloat16 or wider, within the bound.
No kernel may reach another device: no remote copies, remote signals or barrier semaphores. Data moves between devices by JAX's collectives and lax.ppermute only.
A program may use at most 64 MiB of HBM per device.

v0:
```python
import jax
import jax.numpy as jnp
from jax import lax
from jax.sharding import PartitionSpec as P

DITHER = 256


def extended(cells, sides, width):
    for axis, dim in sides:
        count = lax.axis_size(axis)
        ends = count - 1
        head = lax.slice_in_dim(cells, 0, width, axis=dim)
        tail = lax.slice_in_dim(cells, cells.shape[dim] - width, cells.shape[dim], axis=dim)
        cells = jnp.concatenate(
            [
                lax.ppermute(tail, axis, [(i, (i + 1) % count) for i in range(ends)]),
                cells,
                lax.ppermute(head, axis, [((i + 1) % count, i) for i in range(ends)]),
            ],
            axis=dim,
        )
    return cells


def tap_table(tap_values, out_count, in_count):
    offsets = (
        jnp.arange(in_count, dtype=jnp.int32)[None, :]
        - jnp.arange(out_count, dtype=jnp.int32)[:, None]
    )
    picks = (
        offsets[:, :, None] == jnp.arange(tap_values.shape[1], dtype=jnp.int32)[None, None, :]
    ).astype(jnp.bfloat16)
    return jnp.einsum("kt,oit->koi", tap_values, picks, preferred_element_type=jnp.float32).astype(
        jnp.bfloat16
    )


def batch_terms(
    padded,
    inv_block,
    coef_block,
    offsets,
    covered,
    row_first,
    row_table,
    col_table,
    total_rows,
    total_cols,
):
    visit_count, row_count, col_count = inv_block.shape
    block_count = -(-col_count // 128)
    span_cols = padded.shape[2]
    padded = jnp.pad(padded, ((0, 0), (0, 0), (0, (block_count + 1) * 128 - span_cols)))
    col_ids = jnp.arange(col_count, dtype=jnp.int32)
    row_ids = row_first + jnp.arange(row_count, dtype=jnp.int32)
    col_coord = (2.0 * col_ids.astype(jnp.float32) + 1.0) / total_cols - 1.0
    row_coord = (2.0 * row_ids.astype(jnp.float32) + 1.0) / total_rows - 1.0

    def one_basis(which, matched):
        row_kernel = lax.dynamic_index_in_dim(row_table, which, 0, keepdims=False)
        col_kernel = lax.dynamic_index_in_dim(col_table, which, 0, keepdims=False)
        passed = jnp.einsum(
            "ij,vjx->ivx", row_kernel, padded, preferred_element_type=jnp.float32
        ).astype(jnp.bfloat16)
        pieces = passed.reshape(row_count, visit_count, block_count + 1, 128)
        lower_part = jnp.einsum(
            "rvbj,ij->rvbi", pieces, col_kernel[:, :128], preferred_element_type=jnp.float32
        )
        upper_part = jnp.einsum(
            "rvbj,ij->rvbi", pieces, col_kernel[:, 128:], preferred_element_type=jnp.float32
        )
        basis_image = lower_part[:, :, :-1] + upper_part[:, :, 1:]
        basis_image = basis_image.reshape(row_count, visit_count, block_count * 128)
        coef_now = lax.dynamic_index_in_dim(coef_block, which, 1, keepdims=False)
        spatial = (
            coef_now[None, :, 0, None]
            + coef_now[None, :, 1, None] * col_coord[None, None, :]
            + coef_now[None, :, 2, None] * row_coord[:, None, None]
        )
        return matched + spatial * basis_image

    starting = jnp.zeros((row_count, visit_count, col_count), jnp.float32)
    matched = lax.fori_loop(0, row_table.shape[0], one_basis, starting)
    inside = (col_ids[None, :] >= offsets[:, None]) & (
        col_ids[None, :] < offsets[:, None] + total_cols - DITHER
    )
    weight = (
        inv_block.astype(jnp.float32)
        * inside[:, None, :].astype(jnp.float32)
        * covered[:, None, None].astype(jnp.float32)
    )
    weight = jnp.transpose(weight, (1, 0, 2))
    return (jnp.sum(weight * matched, axis=1), jnp.sum(weight, axis=1))


def local(images, inv_var, row_taps, col_taps, coeffs, dithers, depths):
    visit_count, row_count, col_count = images.shape
    half_taps = row_taps.shape[1] // 2
    sky_index = lax.axis_index("sky")
    tile_count = lax.axis_size("sky")
    group_index = lax.axis_index("visit")
    group_count = lax.axis_size("visit")
    visits_all = visit_count * group_count
    first_visit = sky_index * visits_all // tile_count
    tile_depth = depths[0]
    total_rows = row_count * tile_count
    row_first = sky_index * row_count
    row_table = tap_table(row_taps, row_count, row_count + 2 * half_taps)
    col_table = tap_table(col_taps, 128, 256)
    padded = extended(images, (("sky", 1),), half_taps)
    padded = jnp.pad(padded, ((0, 0), (0, 0), (half_taps, half_taps)))
    visit_order = group_index * visit_count + jnp.arange(visit_count, dtype=jnp.int32)
    covered = jnp.mod(visit_order - first_visit, visits_all) < tile_depth
    coef_block = lax.dynamic_slice_in_dim(coeffs, group_index * visit_count, visit_count, 0)
    offsets = lax.dynamic_slice_in_dim(dithers, group_index * visit_count, visit_count, 0)
    partial_value = batch_terms(
        padded,
        inv_var,
        coef_block,
        offsets,
        covered,
        row_first,
        row_table,
        col_table,
        total_rows,
        col_count,
    )
    numerator, denominator = (
        lax.psum_scatter(partial_value[0], "visit", scatter_dimension=1, tiled=True),
        lax.psum_scatter(partial_value[1], "visit", scatter_dimension=1, tiled=True),
    )
    return numerator / (1.0 + denominator)


def solution(mesh):
    placed = (P("visit", "sky", None), P("visit", "sky", None), P(), P(), P(), P(), P("sky"))
    return jax.shard_map(
        local, mesh=mesh, in_specs=placed, out_specs=P("sky", "visit"), check_vma=False
    )
```

profile of v0, /device:TPU:24, one launch (start us, length us, event | category | flops | bytes accessed | tf_op | source)
XLA Modules:
  0.0 302.3 jit_solution(14467769975356416754)
XLA Ops:
  9.4 4.3 %collective-permute-start.1 = (bf16[8,20,2048]{2,0,1:T(8,128)(2,1)}, bf16[8,20,2048]{2,0,1:T(8,128)(2,1)}, u32[]{:S(2)}, u32[]{:S(2)}) collective-permute-start(bf16[8,20,2048]{2,0,1:T(8,128)(2,1)} %copy.28), channel_id=1, source_target_pairs={{4,0},{8,4},{12,8},{16,12},{20,16},{24,20},{28,24},{32,28},{36,32}... | collective-permute-start | bytes 1966088 | tf_op jit(solution)/shard_map/ppermute | solution.py:19
  26.5 2.7 collective-permute-done
  30.7 4.0 %fusion.23 = bf16[8,136,2088]{2,1,0:T(8,128)(2,1)S(1)} fusion(bf16[8,20,2048]{2,1,0:T(8,128)(2,1)S(1)} %copy.22, bf16[8,96,2048]{2,1,0:T(8,128)(2,1)S(1)} %copy-done.2, bf16[8,20,2048]{2,1,0:T(8,128)(2,1)S(1)} %copy.21), kind=kLoop, calls=%fused_computation.38 | loop fusion | flops 27260928 | bytes 8999936 | tf_op jit(solution)/shard_map/concatenate | solution.py:15
  37.3 199.8 %while.14 = (s32[]{:T(128)}, f32[96,8,2048]{2,1,0:T(8,128)}, f32[8,11,3]{0,2,1:T(4,128)}, bf16[11,96,136]{1,2,0:T(8,128)(2,1)S(1)}, bf16[8,136,2176]{2,1,0:T(8,1...) while((s32[]{:T(128)}, f32[96,8,2048]{2,1,0:T(8,128)}, ...), condition=%wide.region_1.2_spmd.clone, body=%wide.region_0.1_spmd.clone.sunk | while | flops 1269443840 | bytes 84400552 | solution.py:84
  39.1 3.6 %convolution_convert_fusion.2 = bf16[96,8,2176]{2,0,1:T(8,128)(2,1)S(1)} fusion(bf16[8,136,2176]{2,1,0:T(8,128)(2,1)} %get-tuple-element.289, bf16[11,96,136]{1,2,0:T(8,128)(2,1)S(1)} %get-tuple-element.288, s32[]{:T(128)S(6)} %copy.47), kind=kOutput, calls=%fused_computation.4.clone.1 | convolution fusion | flops 456228864 | bytes 8112132 | tf_op jit(solution)/shard_map/while/body/eval_jaxpr/ij,vjx->ivx/dot_general | solution.py:63
  42.7 3.9 %fusion.48 = f32[96,8,16,128]{3,1,2,0:T(8,128)S(1)} fusion(bf16[96,8,2176]{2,0,1:T(8,128)(2,1)S(1)} %convolution_convert_fusion.2, bf16[128,256]{1,0:T(8,128)(2,1)S(1)} %dynamic-slice_bitcast_fusion.4), kind=kOutput, calls=%fused_computation.5.clone.1 | convolution fusion | flops 402653184 | bytes 9666560 | tf_op jit(solution)/shard_map/while/body/eval_jaxpr/slice | solution.py:73
  46.7 6.2 %fusion.49 = f32[96,8,2048]{2,1,0:T(8,128)S(1)} fusion(f32[96,8,2048]{2,1,0:T(8,128)S(1)} %bitcast.74, f32[96,8,16,128]{3,1,2,0:T(8,128)S(1)} %fusion.48, f32[96,8]{1,0:T(8,128)S(1)} %broadcast_multiply_fusion.2, f32[8,2048]{1,0:T(8,128)S(1)} %multiply_add_fusion.8, pred[]{:T(512)S(6)} %compare.51, ...), kind=kOutput, calls=%fused_computation.3.clone.1 | convolution fusion | flops 410517504 | bytes 22364160 | tf_op jit(solution)/shard_map/while/body/eval_jaxpr/slice | solution.py:73
  52.9 2.7 copy-done.1
  57.3 3.6 %convolution_convert_fusion.2 = bf16[96,8,2176]{2,0,1:T(8,128)(2,1)S(1)} fusion(bf16[8,136,2176]{2,1,0:T(8,128)(2,1)} %get-tuple-element.289, bf16[11,96,136]{1,2,0:T(8,128)(2,1)S(1)} %get-tuple-element.288, s32[]{:T(128)S(6)} %copy.47), kind=kOutput, calls=%fused_computation.4.clone.1 | convolution fusion | flops 456228864 | bytes 8112132 | tf_op jit(solution)/shard_map/while/body/eval_jaxpr/ij,vjx->ivx/dot_general | solution.py:63
  60.9 3.9 %fusion.48 = f32[96,8,16,128]{3,1,2,0:T(8,128)S(1)} fusion(bf16[96,8,2176]{2,0,1:T(8,128)(2,1)S(1)} %convolution_convert_fusion.2, bf16[128,256]{1,0:T(8,128)(2,1)S(1)} %dynamic-slice_bitcast_fusion.4), kind=kOutput, calls=%fused_computation.5.clone.1 | convolution fusion | flops 402653184 | bytes 9666560 | tf_op jit(solution)/shard_map/while/body/eval_jaxpr/slice | solution.py:73
  64.9 6.2 %fusion.49 = f32[96,8,2048]{2,1,0:T(8,128)S(1)} fusion(f32[96,8,2048]{2,1,0:T(8,128)S(1)} %bitcast.74, f32[96,8,16,128]{3,1,2,0:T(8,128)S(1)} %fusion.48, f32[96,8]{1,0:T(8,128)S(1)} %broadcast_multiply_fusion.2, f32[8,2048]{1,0:T(8,128)S(1)} %multiply_add_fusion.8, pred[]{:T(512)S(6)} %compare.51, ...), kind=kOutput, calls=%fused_computation.3.clone.1 | convolution fusion | flops 410517504 | bytes 22364160 | tf_op jit(solution)/shard_map/while/body/eval_jaxpr/slice | solution.py:73
  71.1 2.7 copy-done.1
  75.5 3.6 %convolution_convert_fusion.2 = bf16[96,8,2176]{2,0,1:T(8,128)(2,1)S(1)} fusion(bf16[8,136,2176]{2,1,0:T(8,128)(2,1)} %get-tuple-element.289, bf16[11,96,136]{1,2,0:T(8,128)(2,1)S(1)} %get-tuple-element.288, s32[]{:T(128)S(6)} %copy.47), kind=kOutput, calls=%fused_computation.4.clone.1 | convolution fusion | flops 456228864 | bytes 8112132 | tf_op jit(solution)/shard_map/while/body/eval_jaxpr/ij,vjx->ivx/dot_general | solution.py:63
  79.1 3.9 %fusion.48 = f32[96,8,16,128]{3,1,2,0:T(8,128)S(1)} fusion(bf16[96,8,2176]{2,0,1:T(8,128)(2,1)S(1)} %convolution_convert_fusion.2, bf16[128,256]{1,0:T(8,128)(2,1)S(1)} %dynamic-slice_bitcast_fusion.4), kind=kOutput, calls=%fused_computation.5.clone.1 | convolution fusion | flops 402653184 | bytes 9666560 | tf_op jit(solution)/shard_map/while/body/eval_jaxpr/slice | solution.py:73
  83.0 6.2 %fusion.49 = f32[96,8,2048]{2,1,0:T(8,128)S(1)} fusion(f32[96,8,2048]{2,1,0:T(8,128)S(1)} %bitcast.74, f32[96,8,16,128]{3,1,2,0:T(8,128)S(1)} %fusion.48, f32[96,8]{1,0:T(8,128)S(1)} %broadcast_multiply_fusion.2, f32[8,2048]{1,0:T(8,128)S(1)} %multiply_add_fusion.8, pred[]{:T(512)S(6)} %compare.51, ...), kind=kOutput, calls=%fused_computation.3.clone.1 | convolution fusion | flops 410517504 | bytes 22364160 | tf_op jit(solution)/shard_map/while/body/eval_jaxpr/slice | solution.py:73
  89.3 2.7 copy-done.1
  93.6 3.6 %convolution_convert_fusion.2 = bf16[96,8,2176]{2,0,1:T(8,128)(2,1)S(1)} fusion(bf16[8,136,2176]{2,1,0:T(8,128)(2,1)} %get-tuple-element.289, bf16[11,96,136]{1,2,0:T(8,128)(2,1)S(1)} %get-tuple-element.288, s32[]{:T(128)S(6)} %copy.47), kind=kOutput, calls=%fused_computation.4.clone.1 | convolution fusion | flops 456228864 | bytes 8112132 | tf_op jit(solution)/shard_map/while/body/eval_jaxpr/ij,vjx->ivx/dot_general | solution.py:63
  97.2 3.9 %fusion.48 = f32[96,8,16,128]{3,1,2,0:T(8,128)S(1)} fusion(bf16[96,8,2176]{2,0,1:T(8,128)(2,1)S(1)} %convolution_convert_fusion.2, bf16[128,256]{1,0:T(8,128)(2,1)S(1)} %dynamic-slice_bitcast_fusion.4), kind=kOutput, calls=%fused_computation.5.clone.1 | convolution fusion | flops 402653184 | bytes 9666560 | tf_op jit(solution)/shard_map/while/body/eval_jaxpr/slice | solution.py:73
  101.2 6.2 %fusion.49 = f32[96,8,2048]{2,1,0:T(8,128)S(1)} fusion(f32[96,8,2048]{2,1,0:T(8,128)S(1)} %bitcast.74, f32[96,8,16,128]{3,1,2,0:T(8,128)S(1)} %fusion.48, f32[96,8]{1,0:T(8,128)S(1)} %broadcast_multiply_fusion.2, f32[8,2048]{1,0:T(8,128)S(1)} %multiply_add_fusion.8, pred[]{:T(512)S(6)} %compare.51, ...), kind=kOutput, calls=%fused_computation.3.clone.1 | convolution fusion | flops 410517504 | bytes 22364160 | tf_op jit(solution)/shard_map/while/body/eval_jaxpr/slice | solution.py:73
  107.4 2.7 copy-done.1
  111.7 3.6 %convolution_convert_fusion.2 = bf16[96,8,2176]{2,0,1:T(8,128)(2,1)S(1)} fusion(bf16[8,136,2176]{2,1,0:T(8,128)(2,1)} %get-tuple-element.289, bf16[11,96,136]{1,2,0:T(8,128)(2,1)S(1)} %get-tuple-element.288, s32[]{:T(128)S(6)} %copy.47), kind=kOutput, calls=%fused_computation.4.clone.1 | convolution fusion | flops 456228864 | bytes 8112132 | tf_op jit(solution)/shard_map/while/body/eval_jaxpr/ij,vjx->ivx/dot_general | solution.py:63
  115.3 3.9 %fusion.48 = f32[96,8,16,128]{3,1,2,0:T(8,128)S(1)} fusion(bf16[96,8,2176]{2,0,1:T(8,128)(2,1)S(1)} %convolution_convert_fusion.2, bf16[128,256]{1,0:T(8,128)(2,1)S(1)} %dynamic-slice_bitcast_fusion.4), kind=kOutput, calls=%fused_computation.5.clone.1 | convolution fusion | flops 402653184 | bytes 9666560 | tf_op jit(solution)/shard_map/while/body/eval_jaxpr/slice | solution.py:73
  119.3 6.2 %fusion.49 = f32[96,8,2048]{2,1,0:T(8,128)S(1)} fusion(f32[96,8,2048]{2,1,0:T(8,128)S(1)} %bitcast.74, f32[96,8,16,128]{3,1,2,0:T(8,128)S(1)} %fusion.48, f32[96,8]{1,0:T(8,128)S(1)} %broadcast_multiply_fusion.2, f32[8,2048]{1,0:T(8,128)S(1)} %multiply_add_fusion.8, pred[]{:T(512)S(6)} %compare.51, ...), kind=kOutput, calls=%fused_computation.3.clone.1 | convolution fusion | flops 410517504 | bytes 22364160 | tf_op jit(solution)/shard_map/while/body/eval_jaxpr/slice | solution.py:73
  125.5 2.7 copy-done.1
  129.9 3.6 %convolution_convert_fusion.2 = bf16[96,8,2176]{2,0,1:T(8,128)(2,1)S(1)} fusion(bf16[8,136,2176]{2,1,0:T(8,128)(2,1)} %get-tuple-element.289, bf16[11,96,136]{1,2,0:T(8,128)(2,1)S(1)} %get-tuple-element.288, s32[]{:T(128)S(6)} %copy.47), kind=kOutput, calls=%fused_computation.4.clone.1 | convolution fusion | flops 456228864 | bytes 8112132 | tf_op jit(solution)/shard_map/while/body/eval_jaxpr/ij,vjx->ivx/dot_general | solution.py:63
  133.5 3.9 %fusion.48 = f32[96,8,16,128]{3,1,2,0:T(8,128)S(1)} fusion(bf16[96,8,2176]{2,0,1:T(8,128)(2,1)S(1)} %convolution_convert_fusion.2, bf16[128,256]{1,0:T(8,128)(2,1)S(1)} %dynamic-slice_bitcast_fusion.4), kind=kOutput, calls=%fused_computation.5.clone.1 | convolution fusion | flops 402653184 | bytes 9666560 | tf_op jit(solution)/shard_map/while/body/eval_jaxpr/slice | solution.py:73
  137.4 6.2 %fusion.49 = f32[96,8,2048]{2,1,0:T(8,128)S(1)} fusion(f32[96,8,2048]{2,1,0:T(8,128)S(1)} %bitcast.74, f32[96,8,16,128]{3,1,2,0:T(8,128)S(1)} %fusion.48, f32[96,8]{1,0:T(8,128)S(1)} %broadcast_multiply_fusion.2, f32[8,2048]{1,0:T(8,128)S(1)} %multiply_add_fusion.8, pred[]{:T(512)S(6)} %compare.51, ...), kind=kOutput, calls=%fused_computation.3.clone.1 | convolution fusion | flops 410517504 | bytes 22364160 | tf_op jit(solution)/shard_map/while/body/eval_jaxpr/slice | solution.py:73
  148.0 3.6 %convolution_convert_fusion.2 = bf16[96,8,2176]{2,0,1:T(8,128)(2,1)S(1)} fusion(bf16[8,136,2176]{2,1,0:T(8,128)(2,1)} %get-tuple-element.289, bf16[11,96,136]{1,2,0:T(8,128)(2,1)S(1)} %get-tuple-element.288, s32[]{:T(128)S(6)} %copy.47), kind=kOutput, calls=%fused_computation.4.clone.1 | convolution fusion | flops 456228864 | bytes 8112132 | tf_op jit(solution)/shard_map/while/body/eval_jaxpr/ij,vjx->ivx/dot_general | solution.py:63
  151.6 3.9 %fusion.48 = f32[96,8,16,128]{3,1,2,0:T(8,128)S(1)} fusion(bf16[96,8,2176]{2,0,1:T(8,128)(2,1)S(1)} %convolution_convert_fusion.2, bf16[128,256]{1,0:T(8,128)(2,1)S(1)} %dynamic-slice_bitcast_fusion.4), kind=kOutput, calls=%fused_computation.5.clone.1 | convolution fusion | flops 402653184 | bytes 9666560 | tf_op jit(solution)/shard_map/while/body/eval_jaxpr/slice | solution.py:73
  155.6 6.2 %fusion.49 = f32[96,8,2048]{2,1,0:T(8,128)S(1)} fusion(f32[96,8,2048]{2,1,0:T(8,128)S(1)} %bitcast.74, f32[96,8,16,128]{3,1,2,0:T(8,128)S(1)} %fusion.48, f32[96,8]{1,0:T(8,128)S(1)} %broadcast_multiply_fusion.2, f32[8,2048]{1,0:T(8,128)S(1)} %multiply_add_fusion.8, pred[]{:T(512)S(6)} %compare.51, ...), kind=kOutput, calls=%fused_computation.3.clone.1 | convolution fusion | flops 410517504 | bytes 22364160 | tf_op jit(solution)/shard_map/while/body/eval_jaxpr/slice | solution.py:73
  161.8 2.7 copy-done.1
  166.2 3.6 %convolution_convert_fusion.2 = bf16[96,8,2176]{2,0,1:T(8,128)(2,1)S(1)} fusion(bf16[8,136,2176]{2,1,0:T(8,128)(2,1)} %get-tuple-element.289, bf16[11,96,136]{1,2,0:T(8,128)(2,1)S(1)} %get-tuple-element.288, s32[]{:T(128)S(6)} %copy.47), kind=kOutput, calls=%fused_computation.4.clone.1 | convolution fusion | flops 456228864 | bytes 8112132 | tf_op jit(solution)/shard_map/while/body/eval_jaxpr/ij,vjx->ivx/dot_general | solution.py:63
  169.8 3.9 %fusion.48 = f32[96,8,16,128]{3,1,2,0:T(8,128)S(1)} fusion(bf16[96,8,2176]{2,0,1:T(8,128)(2,1)S(1)} %convolution_convert_fusion.2, bf16[128,256]{1,0:T(8,128)(2,1)S(1)} %dynamic-slice_bitcast_fusion.4), kind=kOutput, calls=%fused_computation.5.clone.1 | convolution fusion | flops 402653184 | bytes 9666560 | tf_op jit(solution)/shard_map/while/body/eval_jaxpr/slice | solution.py:73
  173.7 6.2 %fusion.49 = f32[96,8,2048]{2,1,0:T(8,128)S(1)} fusion(f32[96,8,2048]{2,1,0:T(8,128)S(1)} %bitcast.74, f32[96,8,16,128]{3,1,2,0:T(8,128)S(1)} %fusion.48, f32[96,8]{1,0:T(8,128)S(1)} %broadcast_multiply_fusion.2, f32[8,2048]{1,0:T(8,128)S(1)} %multiply_add_fusion.8, pred[]{:T(512)S(6)} %compare.51, ...), kind=kOutput, calls=%fused_computation.3.clone.1 | convolution fusion | flops 410517504 | bytes 22364160 | tf_op jit(solution)/shard_map/while/body/eval_jaxpr/slice | solution.py:73
  180.0 2.7 copy-done.1
  184.3 3.6 %convolution_convert_fusion.2 = bf16[96,8,2176]{2,0,1:T(8,128)(2,1)S(1)} fusion(bf16[8,136,2176]{2,1,0:T(8,128)(2,1)} %get-tuple-element.289, bf16[11,96,136]{1,2,0:T(8,128)(2,1)S(1)} %get-tuple-element.288, s32[]{:T(128)S(6)} %copy.47), kind=kOutput, calls=%fused_computation.4.clone.1 | convolution fusion | flops 456228864 | bytes 8112132 | tf_op jit(solution)/shard_map/while/body/eval_jaxpr/ij,vjx->ivx/dot_general | solution.py:63
  187.9 3.9 %fusion.48 = f32[96,8,16,128]{3,1,2,0:T(8,128)S(1)} fusion(bf16[96,8,2176]{2,0,1:T(8,128)(2,1)S(1)} %convolution_convert_fusion.2, bf16[128,256]{1,0:T(8,128)(2,1)S(1)} %dynamic-slice_bitcast_fusion.4), kind=kOutput, calls=%fused_computation.5.clone.1 | convolution fusion | flops 402653184 | bytes 9666560 | tf_op jit(solution)/shard_map/while/body/eval_jaxpr/slice | solution.py:73
  191.9 6.2 %fusion.49 = f32[96,8,2048]{2,1,0:T(8,128)S(1)} fusion(f32[96,8,2048]{2,1,0:T(8,128)S(1)} %bitcast.74, f32[96,8,16,128]{3,1,2,0:T(8,128)S(1)} %fusion.48, f32[96,8]{1,0:T(8,128)S(1)} %broadcast_multiply_fusion.2, f32[8,2048]{1,0:T(8,128)S(1)} %multiply_add_fusion.8, pred[]{:T(512)S(6)} %compare.51, ...), kind=kOutput, calls=%fused_computation.3.clone.1 | convolution fusion | flops 410517504 | bytes 22364160 | tf_op jit(solution)/shard_map/while/body/eval_jaxpr/slice | solution.py:73
  198.2 2.7 copy-done.1
  202.4 3.6 %convolution_convert_fusion.2 = bf16[96,8,2176]{2,0,1:T(8,128)(2,1)S(1)} fusion(bf16[8,136,2176]{2,1,0:T(8,128)(2,1)} %get-tuple-element.289, bf16[11,96,136]{1,2,0:T(8,128)(2,1)S(1)} %get-tuple-element.288, s32[]{:T(128)S(6)} %copy.47), kind=kOutput, calls=%fused_computation.4.clone.1 | convolution fusion | flops 456228864 | bytes 8112132 | tf_op jit(solution)/shard_map/while/body/eval_jaxpr/ij,vjx->ivx/dot_general | solution.py:63
  206.0 3.9 %fusion.48 = f32[96,8,16,128]{3,1,2,0:T(8,128)S(1)} fusion(bf16[96,8,2176]{2,0,1:T(8,128)(2,1)S(1)} %convolution_convert_fusion.2, bf16[128,256]{1,0:T(8,128)(2,1)S(1)} %dynamic-slice_bitcast_fusion.4), kind=kOutput, calls=%fused_computation.5.clone.1 | convolution fusion | flops 402653184 | bytes 9666560 | tf_op jit(solution)/shard_map/while/body/eval_jaxpr/slice | solution.py:73
  210.0 6.2 %fusion.49 = f32[96,8,2048]{2,1,0:T(8,128)S(1)} fusion(f32[96,8,2048]{2,1,0:T(8,128)S(1)} %bitcast.74, f32[96,8,16,128]{3,1,2,0:T(8,128)S(1)} %fusion.48, f32[96,8]{1,0:T(8,128)S(1)} %broadcast_multiply_fusion.2, f32[8,2048]{1,0:T(8,128)S(1)} %multiply_add_fusion.8, pred[]{:T(512)S(6)} %compare.51, ...), kind=kOutput, calls=%fused_computation.3.clone.1 | convolution fusion | flops 410517504 | bytes 22364160 | tf_op jit(solution)/shard_map/while/body/eval_jaxpr/slice | solution.py:73
  220.6 3.6 %convolution_convert_fusion.2 = bf16[96,8,2176]{2,0,1:T(8,128)(2,1)S(1)} fusion(bf16[8,136,2176]{2,1,0:T(8,128)(2,1)} %get-tuple-element.289, bf16[11,96,136]{1,2,0:T(8,128)(2,1)S(1)} %get-tuple-element.288, s32[]{:T(128)S(6)} %copy.47), kind=kOutput, calls=%fused_computation.4.clone.1 | convolution fusion | flops 456228864 | bytes 8112132 | tf_op jit(solution)/shard_map/while/body/eval_jaxpr/ij,vjx->ivx/dot_general | solution.py:63
  224.2 3.9 %fusion.48 = f32[96,8,16,128]{3,1,2,0:T(8,128)S(1)} fusion(bf16[96,8,2176]{2,0,1:T(8,128)(2,1)S(1)} %convolution_convert_fusion.2, bf16[128,256]{1,0:T(8,128)(2,1)S(1)} %dynamic-slice_bitcast_fusion.4), kind=kOutput, calls=%fused_computation.5.clone.1 | convolution fusion | flops 402653184 | bytes 9666560 | tf_op jit(solution)/shard_map/while/body/eval_jaxpr/slice | solution.py:73
  228.2 6.2 %fusion.49 = f32[96,8,2048]{2,1,0:T(8,128)S(1)} fusion(f32[96,8,2048]{2,1,0:T(8,128)S(1)} %bitcast.74, f32[96,8,16,128]{3,1,2,0:T(8,128)S(1)} %fusion.48, f32[96,8]{1,0:T(8,128)S(1)} %broadcast_multiply_fusion.2, f32[8,2048]{1,0:T(8,128)S(1)} %multiply_add_fusion.8, pred[]{:T(512)S(6)} %compare.51, ...), kind=kOutput, calls=%fused_computation.3.clone.1 | convolution fusion | flops 410517504 | bytes 22364160 | tf_op jit(solution)/shard_map/while/body/eval_jaxpr/slice | solution.py:73
  237.1 9.0 %bitcast_reduce_fusion = (f32[96,2048]{1,0:T(8,128)}, f32[96,2048]{1,0:T(8,128)}) fusion(f32[8]{0:T(128)} %compare_convert_fusion, f32[8,2048]{1,0:T(8,128)} %fusion.32, bf16[8,96,2048]{2,1,0:T(8,128)(2,1)S(1)} %copy-done.3, f32[96,8,2048]{2,1,0:T(8,128)} %get-tuple-element.144), kind=kLoop, calls=%fused_computation.28 | loop fusion | flops 9043968 | bytes 11075616 | tf_op jit(solution)/shard_map/reduce_sum | solution.py:94
  246.9 22.1 %reduce-scatter.5.cloned.1.call-done = f32[96,512]{1,0:T(8,128)} async-done(((f32[96,2048]{1,0:T(8,128)}), f32[96,512]{1,0:T(8,128)}) %reduce-scatter.5.cloned.1.call-update) | async-done | bytes 196624 | tf_op jit(solution)/shard_map/reduce_scatter | solution.py:131
  269.0 24.7 %reduce-scatter.3.cloned.1.call-done = f32[96,512]{1,0:T(8,128)} async-done(((f32[96,2048]{1,0:T(8,128)}), f32[96,512]{1,0:T(8,128)}) %reduce-scatter.3.cloned.1.call-update) | async-done | bytes 196624 | tf_op jit(solution)/shard_map/reduce_scatter | solution.py:130
  (178 shorter events, 48.2 us)
Async XLA Ops:
  6.5 17.1 %copy-start = (f32[32,11,3]{0,2,1:T(4,128)S(1)}, f32[32,11,3]{0,2,1:T(4,128)}, u32[]{:S(2)}) copy-start(f32[32,11,3]{0,2,1:T(4,128)} %param.13) | copy-start | bytes 12676
  6.5 11.6 %copy-start.4 = (bf16[11,41]{1,0:T(8,128)(2,1)S(1)}, bf16[11,41]{1,0:T(8,128)(2,1)}, u32[]{:S(2)}) copy-start(bf16[11,41]{1,0:T(8,128)(2,1)} %param.11) | copy-start | bytes 2710
  6.5 262.4 %reduce-scatter.5.cloned.1.call-start = ((), (), s32[]{:S(2)}) async-start(), calls=%async_computation.3 | async-start | bytes 983040 | tf_op jit(solution)/shard_map/reduce_scatter | solution.py:131
  9.4 15.7 %collective-permute-start.1 = (bf16[8,20,2048]{2,0,1:T(8,128)(2,1)}, bf16[8,20,2048]{2,0,1:T(8,128)(2,1)}, u32[]{:S(2)}, u32[]{:S(2)}) collective-permute-start(bf16[8,20,2048]{2,0,1:T(8,128)(2,1)} %copy.28), channel_id=1, source_target_pairs={{4,0},{8,4},{12,8},{16,12},{20,16},{24,20},{28,24},{32,28},{36,32}... | collective-permute-start | bytes 1966088 | tf_op jit(solution)/shard_map/ppermute | solution.py:19
  13.6 17.0 %copy-start.2 = (bf16[8,96,2048]{2,1,0:T(8,128)(2,1)S(1)}, bf16[8,96,2048]{2,1,0:T(8,128)(2,1)}, u32[]{:S(2)}) copy-start(bf16[8,96,2048]{2,1,0:T(8,128)(2,1)} %param.9) | copy-start | bytes 9437188
  14.9 14.3 %collective-permute-start = (bf16[8,20,2048]{2,0,1:T(8,128)(2,1)}, bf16[8,20,2048]{2,0,1:T(8,128)(2,1)}, u32[]{:S(2)}, u32[]{:S(2)}) collective-permute-start(bf16[8,20,2048]{2,0,1:T(8,128)(2,1)} %copy.27), channel_id=1, source_target_pairs={{0,4},{4,8},{8,12},{12,16},{16,20},{20,24},{24,28},{28,32},{32,36}... | collective-permute-start | bytes 1966088 | tf_op jit(solution)/shard_map/ppermute | solution.py:17
  37.3 199.8 %copy-start.3 = (bf16[8,96,2048]{2,1,0:T(8,128)(2,1)S(1)}, bf16[8,96,2048]{2,1,0:T(8,128)(2,1)}, u32[]{:S(2)}) copy-start(bf16[8,96,2048]{2,1,0:T(8,128)(2,1)} %param.10) | copy-start | bytes 9437188
  39.1 7.6 %slice-start = ((s8[6291456]{0:T(1024)(128)(4,1)}), s8[4194304]{0:T(1024)(128)(4,1)S(1)}, s32[]{:S(2)}) async-start(s8[6291456]{0:T(1024)(128)(4,1)} %bitcast.73), calls=%async_computation.4 | async-start | bytes 8388608 | tf_op jit(solution)/shard_map/while
  42.7 4.0 %slice-start.1 = ((s8[6291456]{0:T(1024)(128)(4,1)}), s8[2097152]{0:T(1024)(128)(4,1)S(1)}, s32[]{:S(2)}) async-start(s8[6291456]{0:T(1024)(128)(4,1)} %bitcast.73), calls=%async_computation.5 | async-start | bytes 4194304 | tf_op jit(solution)/shard_map/while
  52.9 2.7 copy-start.1
  57.3 7.6 %slice-start = ((s8[6291456]{0:T(1024)(128)(4,1)}), s8[4194304]{0:T(1024)(128)(4,1)S(1)}, s32[]{:S(2)}) async-start(s8[6291456]{0:T(1024)(128)(4,1)} %bitcast.73), calls=%async_computation.4 | async-start | bytes 8388608 | tf_op jit(solution)/shard_map/while
  60.9 4.0 %slice-start.1 = ((s8[6291456]{0:T(1024)(128)(4,1)}), s8[2097152]{0:T(1024)(128)(4,1)S(1)}, s32[]{:S(2)}) async-start(s8[6291456]{0:T(1024)(128)(4,1)} %bitcast.73), calls=%async_computation.5 | async-start | bytes 4194304 | tf_op jit(solution)/shard_map/while
  71.1 2.7 copy-start.1
  75.5 7.5 %slice-start = ((s8[6291456]{0:T(1024)(128)(4,1)}), s8[4194304]{0:T(1024)(128)(4,1)S(1)}, s32[]{:S(2)}) async-start(s8[6291456]{0:T(1024)(128)(4,1)} %bitcast.73), calls=%async_computation.4 | async-start | bytes 8388608 | tf_op jit(solution)/shard_map/while
  79.0 4.0 %slice-start.1 = ((s8[6291456]{0:T(1024)(128)(4,1)}), s8[2097152]{0:T(1024)(128)(4,1)S(1)}, s32[]{:S(2)}) async-start(s8[6291456]{0:T(1024)(128)(4,1)} %bitcast.73), calls=%async_computation.5 | async-start | bytes 4194304 | tf_op jit(solution)/shard_map/while
  89.3 2.7 copy-start.1
  93.6 7.5 %slice-start = ((s8[6291456]{0:T(1024)(128)(4,1)}), s8[4194304]{0:T(1024)(128)(4,1)S(1)}, s32[]{:S(2)}) async-start(s8[6291456]{0:T(1024)(128)(4,1)} %bitcast.73), calls=%async_computation.4 | async-start | bytes 8388608 | tf_op jit(solution)/shard_map/while
  97.2 4.0 %slice-start.1 = ((s8[6291456]{0:T(1024)(128)(4,1)}), s8[2097152]{0:T(1024)(128)(4,1)S(1)}, s32[]{:S(2)}) async-start(s8[6291456]{0:T(1024)(128)(4,1)} %bitcast.73), calls=%async_computation.5 | async-start | bytes 4194304 | tf_op jit(solution)/shard_map/while
  107.4 2.7 copy-start.1
  111.7 7.5 %slice-start = ((s8[6291456]{0:T(1024)(128)(4,1)}), s8[4194304]{0:T(1024)(128)(4,1)S(1)}, s32[]{:S(2)}) async-start(s8[6291456]{0:T(1024)(128)(4,1)} %bitcast.73), calls=%async_computation.4 | async-start | bytes 8388608 | tf_op jit(solution)/shard_map/while
  115.3 4.0 %slice-start.1 = ((s8[6291456]{0:T(1024)(128)(4,1)}), s8[2097152]{0:T(1024)(128)(4,1)S(1)}, s32[]{:S(2)}) async-start(s8[6291456]{0:T(1024)(128)(4,1)} %bitcast.73), calls=%async_computation.5 | async-start | bytes 4194304 | tf_op jit(solution)/shard_map/while
  125.5 2.7 copy-start.1
  129.9 7.6 %slice-start = ((s8[6291456]{0:T(1024)(128)(4,1)}), s8[4194304]{0:T(1024)(128)(4,1)S(1)}, s32[]{:S(2)}) async-start(s8[6291456]{0:T(1024)(128)(4,1)} %bitcast.73), calls=%async_computation.4 | async-start | bytes 8388608 | tf_op jit(solution)/shard_map/while
  133.5 4.0 %slice-start.1 = ((s8[6291456]{0:T(1024)(128)(4,1)}), s8[2097152]{0:T(1024)(128)(4,1)S(1)}, s32[]{:S(2)}) async-start(s8[6291456]{0:T(1024)(128)(4,1)} %bitcast.73), calls=%async_computation.5 | async-start | bytes 4194304 | tf_op jit(solution)/shard_map/while
  143.7 2.7 copy-start.1
  148.0 7.5 %slice-start = ((s8[6291456]{0:T(1024)(128)(4,1)}), s8[4194304]{0:T(1024)(128)(4,1)S(1)}, s32[]{:S(2)}) async-start(s8[6291456]{0:T(1024)(128)(4,1)} %bitcast.73), calls=%async_computation.4 | async-start | bytes 8388608 | tf_op jit(solution)/shard_map/while
  151.6 4.0 %slice-start.1 = ((s8[6291456]{0:T(1024)(128)(4,1)}), s8[2097152]{0:T(1024)(128)(4,1)S(1)}, s32[]{:S(2)}) async-start(s8[6291456]{0:T(1024)(128)(4,1)} %bitcast.73), calls=%async_computation.5 | async-start | bytes 4194304 | tf_op jit(solution)/shard_map/while
  161.8 2.7 copy-start.1
  166.2 7.6 %slice-start = ((s8[6291456]{0:T(1024)(128)(4,1)}), s8[4194304]{0:T(1024)(128)(4,1)S(1)}, s32[]{:S(2)}) async-start(s8[6291456]{0:T(1024)(128)(4,1)} %bitcast.73), calls=%async_computation.4 | async-start | bytes 8388608 | tf_op jit(solution)/shard_map/while
  169.8 4.0 %slice-start.1 = ((s8[6291456]{0:T(1024)(128)(4,1)}), s8[2097152]{0:T(1024)(128)(4,1)S(1)}, s32[]{:S(2)}) async-start(s8[6291456]{0:T(1024)(128)(4,1)} %bitcast.73), calls=%async_computation.5 | async-start | bytes 4194304 | tf_op jit(solution)/shard_map/while
  180.0 2.7 copy-start.1
  184.3 7.5 %slice-start = ((s8[6291456]{0:T(1024)(128)(4,1)}), s8[4194304]{0:T(1024)(128)(4,1)S(1)}, s32[]{:S(2)}) async-start(s8[6291456]{0:T(1024)(128)(4,1)} %bitcast.73), calls=%async_computation.4 | async-start | bytes 8388608 | tf_op jit(solution)/shard_map/while
  187.9 4.0 %slice-start.1 = ((s8[6291456]{0:T(1024)(128)(4,1)}), s8[2097152]{0:T(1024)(128)(4,1)S(1)}, s32[]{:S(2)}) async-start(s8[6291456]{0:T(1024)(128)(4,1)} %bitcast.73), calls=%async_computation.5 | async-start | bytes 4194304 | tf_op jit(solution)/shard_map/while
  198.1 2.7 copy-start.1
  202.4 7.5 %slice-start = ((s8[6291456]{0:T(1024)(128)(4,1)}), s8[4194304]{0:T(1024)(128)(4,1)S(1)}, s32[]{:S(2)}) async-start(s8[6291456]{0:T(1024)(128)(4,1)} %bitcast.73), calls=%async_computation.4 | async-start | bytes 8388608 | tf_op jit(solution)/shard_map/while
  206.0 4.0 %slice-start.1 = ((s8[6291456]{0:T(1024)(128)(4,1)}), s8[2097152]{0:T(1024)(128)(4,1)S(1)}, s32[]{:S(2)}) async-start(s8[6291456]{0:T(1024)(128)(4,1)} %bitcast.73), calls=%async_computation.5 | async-start | bytes 4194304 | tf_op jit(solution)/shard_map/while
  216.2 2.7 copy-start.1
  220.6 7.6 %slice-start = ((s8[6291456]{0:T(1024)(128)(4,1)}), s8[4194304]{0:T(1024)(128)(4,1)S(1)}, s32[]{:S(2)}) async-start(s8[6291456]{0:T(1024)(128)(4,1)} %bitcast.73), calls=%async_computation.4 | async-start | bytes 8388608 | tf_op jit(solution)/shard_map/while
  224.2 4.0 %slice-start.1 = ((s8[6291456]{0:T(1024)(128)(4,1)}), s8[2097152]{0:T(1024)(128)(4,1)S(1)}, s32[]{:S(2)}) async-start(s8[6291456]{0:T(1024)(128)(4,1)} %bitcast.73), calls=%async_computation.5 | async-start | bytes 4194304 | tf_op jit(solution)/shard_map/while
  234.4 2.7 copy-start.1
  246.1 47.6 %reduce-scatter.3.cloned.1.call-start = ((), (), s32[]{:S(2)}) async-start(), calls=%async_computation.2 | async-start | bytes 983040 | tf_op jit(solution)/shard_map/reduce_scatter | solution.py:130
Sparse Core Ops, SparseCore 0:
  246.2 22.6 reduce-scatter.4
  271.4 22.2 reduce-scatter.2
where the time goes:
time: 304 us; the launch traced here: 302 us
  matrix products  154 us (51%)
  local copies, waits for them, and re-layouts  57.5 us (19%)
  waiting for transfers between devices  50.3 us (17%)
  other arithmetic  19.3 us (6%)
  between operations  14.2 us (5%)
  starting transfers between devices  6.23 us (2%)
    slice x22, matrix products, one_basis(): basis_image = lower_part[:, :, :-1] + upper_part[:, :, 1:]  112 us
    dot_general x11, matrix products, one_basis(): jnp.einsum('ij,vjx->ivx', row_kernel, padded, preferred_element_type=jnp....  39.4 us
    while x66, local copies, waits for them, and re-layouts  29.3 us
    reduce_scatter x1, waiting for transfers between devices, local(): lax.psum_scatter(partial_value[0], 'visit', scatter_dimension=1, tiled=True)  24.7 us
    reduce_scatter x1, waiting for transfers between devices, local(): lax.psum_scatter(partial_value[1], 'visit', scatter_dimension=1, tiled=True)  22.1 us
    squeeze x11, local copies, waits for them, and re-layouts, one_basis(): col_kernel = lax.dynamic_index_in_dim(col_table, which, 0, keepdims=False)  9.34 us
    reduce_sum x1, other arithmetic, batch_terms(): return (jnp.sum(weight * matched, axis=1), jnp.sum(weight, axis=1))  9.03 us
    squeeze x11, local copies, waits for them, and re-layouts, one_basis(): coef_now = lax.dynamic_index_in_dim(coef_block, which, 1, keepdims=False)  7.4 us
  transfers between devices with their start and end apart: 4, of which 3 were waited for; matrix products, arithmetic and copies ran while one was open for 3% of the time, Pallas kernels for 0%

commit v1 on v0

v1 whole, which is shorter than its diff:
```python
import jax
import jax.numpy as jnp
from jax import lax
from jax.experimental import pallas as pl
from jax.experimental.pallas import tpu as pltpu
from jax.sharding import PartitionSpec as P

DITHER = 256
SIDE = 128
BLOCK = 256


def row_table(row_taps, row_count):
    basis_count, tap_count = row_taps.shape
    half = tap_count // 2
    slot = jnp.arange(row_count + 64, dtype=jnp.int32)
    top_row = jnp.where(slot < row_count + half, slot - row_count - half, 9999)
    bottom_row = jnp.where(slot < row_count + 32 + half, slot - 32, 9999)
    source = jnp.where(
        slot < row_count, slot, jnp.where(slot < row_count + 32, top_row, bottom_row)
    )
    offset = source[None, :] - jnp.arange(row_count, dtype=jnp.int32)[:, None] + half
    picks = (offset[None] == jnp.arange(tap_count, dtype=jnp.int32)[:, None, None]).astype(
        jnp.bfloat16
    )
    table = jnp.einsum("kt,tos->kos", row_taps, picks, preferred_element_type=jnp.float32)
    return table.astype(jnp.bfloat16).reshape(basis_count * row_count, row_count + 64)


def col_table(col_taps):
    tap_count = col_taps.shape[1]
    half = tap_count // 2
    offset = (
        jnp.arange(BLOCK + 2 * SIDE, dtype=jnp.int32)[:, None]
        - SIDE
        + half
        - jnp.arange(BLOCK, dtype=jnp.int32)[None, :]
    )
    picks = (offset[None] == jnp.arange(tap_count, dtype=jnp.int32)[:, None, None]).astype(
        jnp.bfloat16
    )
    table = jnp.einsum("kt,tpx->kpx", col_taps, picks, preferred_element_type=jnp.float32)
    return table.astype(jnp.bfloat16)


def coadd_kernel(
    scalars,
    coeffs,
    images,
    top,
    bottom,
    inv_var,
    rows_ref,
    cols_ref,
    num_ref,
    den_ref,
    source,
    passed,
    matched,
    *,
    total_rows,
):
    visit = pl.program_id(0)
    visit_count = pl.num_programs(0)
    row_count, col_count = num_ref.shape
    basis_count = cols_ref.shape[0]
    half = top.shape[1]
    blocks = col_count // BLOCK
    row_first = scalars[0]

    @pl.when(visit == 0)
    def _():
        source[...] = jnp.zeros_like(source)
        passed[...] = jnp.zeros_like(passed)
        num_ref[...] = jnp.zeros_like(num_ref)
        den_ref[...] = jnp.zeros_like(den_ref)

    covered = scalars[1 + visit]
    shift = scalars[1 + visit_count + visit]

    @pl.when(covered > 0)
    def _():
        source[0:row_count, :] = images[0]
        source[row_count : row_count + half, :] = top[0]
        source[row_count + 32 : row_count + 32 + half, :] = bottom[0]

        def row_step(block, carry):
            at = pl.multiple_of(block * BLOCK, BLOCK)
            out = jnp.dot(
                rows_ref[...], source[:, pl.ds(at, BLOCK)], preferred_element_type=jnp.float32
            )
            passed[:, pl.ds(pl.multiple_of(at + SIDE, SIDE), BLOCK)] = out.astype(jnp.bfloat16)
            return carry

        lax.fori_loop(0, blocks, row_step, 0)
        matched[...] = jnp.zeros_like(matched)
        row_ids = row_first + lax.broadcasted_iota(jnp.int32, (row_count, 128), 0)
        row_coord = (2.0 * row_ids.astype(jnp.float32) + 1.0) / total_rows - 1.0
        col_ids = lax.broadcasted_iota(jnp.int32, (8, col_count), 1)
        col_coord = (2.0 * col_ids.astype(jnp.float32) + 1.0) / col_count - 1.0

        def col_step(basis, carry):
            first = pl.multiple_of(basis * row_count, row_count)
            lhs = jnp.concatenate(
                [
                    passed[pl.ds(first, row_count), b * BLOCK : (b + 2) * BLOCK]
                    for b in range(blocks)
                ],
                axis=0,
            )
            image = jnp.dot(lhs, cols_ref[basis], preferred_element_type=jnp.float32)
            at = (visit * basis_count + basis) * 3
            row_part = coeffs[at] + coeffs[at + 2] * row_coord
            row_part = jnp.concatenate([row_part, row_part], axis=1)
            col_part = coeffs[at + 1] * col_coord
            for b in range(blocks):
                spatial = row_part.reshape(row_count // 8, 8, BLOCK) + col_part[
                    None, :, b * BLOCK : (b + 1) * BLOCK
                ]
                matched[:, b * BLOCK : (b + 1) * BLOCK] += (
                    spatial.reshape(row_count, BLOCK) * image[b * row_count : (b + 1) * row_count]
                )
            return carry

        lax.fori_loop(0, basis_count, col_step, 0)
        inside = (col_ids[0:1] >= shift) & (col_ids[0:1] < shift + (col_count - DITHER))
        weight = inv_var[0].astype(jnp.float32) * inside.astype(jnp.float32)
        num_ref[...] += weight * matched[...]
        den_ref[...] += weight


def partial_sums(scalars, coeffs, images, top, bottom, inv_var, rows, cols, total_rows):
    visit_count, row_count, col_count = images.shape
    half = top.shape[1]
    plane = jax.ShapeDtypeStruct((row_count, col_count), jnp.float32)
    whole = lambda shape: pl.BlockSpec(shape, lambda v, *_: (0,) * len(shape))
    return pl.pallas_call(
        lambda *refs: coadd_kernel(*refs, total_rows=total_rows),
        out_shape=(plane, plane),
        grid_spec=pltpu.PrefetchScalarGridSpec(
            num_scalar_prefetch=2,
            grid=(visit_count,),
            in_specs=[
                pl.BlockSpec((1, row_count, col_count), lambda v, *_: (v, 0, 0)),
                pl.BlockSpec((1, half, col_count), lambda v, *_: (v, 0, 0)),
                pl.BlockSpec((1, half, col_count), lambda v, *_: (v, 0, 0)),
                pl.BlockSpec((1, row_count, col_count), lambda v, *_: (v, 0, 0)),
                whole(rows.shape),
                whole(cols.shape),
            ],
            out_specs=[whole((row_count, col_count))] * 2,
            scratch_shapes=[
                pltpu.VMEM((row_count + 64, col_count), jnp.bfloat16),
                pltpu.VMEM((rows.shape[0], col_count + 2 * SIDE), jnp.bfloat16),
                pltpu.VMEM((row_count, col_count), jnp.float32),
            ],
        ),
        compiler_params=pltpu.CompilerParams(
            dimension_semantics=("arbitrary",), vmem_limit_bytes=60 << 20
        ),
        name="coadd",
    )(scalars, coeffs, images, top, bottom, inv_var, rows, cols)


def local(images, inv_var, row_taps, col_taps, coeffs, dithers, depths):
    visit_count, row_count, col_count = images.shape
    half = row_taps.shape[1] // 2
    sky = lax.axis_index("sky")
    tiles = lax.axis_size("sky")
    group = lax.axis_index("visit")
    visits_all = visit_count * lax.axis_size("visit")
    top = lax.ppermute(
        images[:, row_count - half :], "sky", [(i, i + 1) for i in range(tiles - 1)]
    )
    bottom = lax.ppermute(images[:, :half], "sky", [(i + 1, i) for i in range(tiles - 1)])
    order = group * visit_count + jnp.arange(visit_count, dtype=jnp.int32)
    covered = jnp.mod(order - sky * visits_all // tiles, visits_all) < depths[0]
    shifts = lax.dynamic_slice_in_dim(dithers, group * visit_count, visit_count, 0)
    scalars = jnp.concatenate(
        [(sky * row_count)[None].astype(jnp.int32), covered.astype(jnp.int32), shifts]
    )
    coefs = lax.dynamic_slice_in_dim(coeffs, group * visit_count, visit_count, 0).reshape(-1)
    numerator, denominator = partial_sums(
        scalars,
        coefs,
        images,
        top,
        bottom,
        inv_var,
        row_table(row_taps, row_count),
        col_table(col_taps),
        row_count * tiles,
    )
    numerator = lax.psum_scatter(numerator, "visit", scatter_dimension=1, tiled=True)
    denominator = lax.psum_scatter(denominator, "visit", scatter_dimension=1, tiled=True)
    return numerator / (1.0 + denominator)


def solution(mesh):
    placed = (P("visit", "sky", None), P("visit", "sky", None), P(), P(), P(), P(), P("sky"))
    return jax.shard_map(
        local, mesh=mesh, in_specs=placed, out_specs=P("sky", "visit"), check_vma=False
    )
```

time: 304 us -> 147 us (0.48)
  matrix products: 154 us -> 6.1 us
  local copies, waits for them, and re-layouts: 57.5 us -> 9.92 us
  waiting for transfers between devices: 50.3 us -> 91.1 us
  other arithmetic: 19.3 us -> 2.6 us
  Pallas kernels: 0 us -> 15.5 us
    slice x22 -> x0, matrix products: 112 us -> none  [one_basis(): basis_image = lower_part[:, :, :-1] + upper_part[:, :, 1:]]
    reduce_scatter x2, waiting for transfers between devices: 46.8 us -> 90.4 us  [the longest x1 65.7 us: local(): lax.psum_scatter(numerator, 'visit', scatter_dimension=1, tiled=True)]
    dot_general x13 -> x2, matrix products: 42.3 us -> 6.1 us  [the longest x1 5.24 us: col_table(): jnp.einsum('kt,tpx->kpx', col_taps, picks, preferred_element_type=jnp.flo...]
    while x66 -> x0, local copies, waits for them, and re-layouts: 29.3 us -> none
    squeeze x22 -> x0, local copies, waits for them, and re-layouts: 16.7 us -> none  [the longest x11 9.34 us: one_basis(): col_kernel = lax.dynamic_index_in_dim(col_table, which, 0, keepdims=False)]
    pallas_call x0 -> x1, Pallas kernels: none -> 15.5 us  [partial_sums(): pl.pallas_call(lambda *refs: coadd_kernel(*refs, total_rows=total_rows),...]
    reduce_sum x1 -> x0, other arithmetic: 9.03 us -> none  [batch_terms(): return (jnp.sum(weight * matched, axis=1), jnp.sum(weight, axis=1))]
    concatenate x1, other arithmetic: 4.02 us -> 0.64 us  [local(): jnp.concatenate([(sky * row_count)[None].astype(jnp.int32), covered.astyp...]
  transfers between devices with their start and end apart: 4 -> 4, of which waited for: 3 -> 2; matrix products, arithmetic and copies ran while one was open for 3% -> 9% of each run, Pallas kernels for 0% -> 0%
where the time goes in v1:
time: 147 us
  waiting for transfers between devices  91.1 us (62%)
  Pallas kernels  15.5 us (11%)
  between operations  14.2 us (10%)
  local copies, waits for them, and re-layouts  9.92 us (7%)
  starting transfers between devices  7.72 us (5%)
  matrix products  6.1 us (4%)
  other arithmetic  2.6 us (2%)
    reduce_scatter x1, waiting for transfers between devices, local(): lax.psum_scatter(numerator, 'visit', scatter_dimension=1, tiled=True)  65.7 us
    reduce_scatter x1, waiting for transfers between devices, local(): lax.psum_scatter(denominator, 'visit', scatter_dimension=1, tiled=True)  24.6 us
    pallas_call x1, Pallas kernels, partial_sums(): pl.pallas_call(lambda *refs: coadd_kernel(*refs, total_rows=total_rows),...  15.5 us
    ppermute x1, starting transfers between devices, local(): lax.ppermute(images[:, :half], 'sky', [(i + 1, i) for i in range(tiles -...  5.75 us
    dot_general x1, matrix products, col_table(): jnp.einsum('kt,tpx->kpx', col_taps, picks, preferred_element_type=jnp.flo...  5.24 us
  transfers between devices with their start and end apart: 4, of which 2 were waited for; matrix products, arithmetic and copies ran while one was open for 9% of the time, Pallas kernels for 0%

profile of v1, /device:TPU:24, one launch (start us, length us, event | category | flops | bytes accessed | tf_op | source)
XLA Modules:
  0.0 147.1 jit_solution(9631147875978516689)
XLA Ops:
  6.5 0.0 copy-start
  6.5 0.0 copy-start.3
  6.5 0.0 copy-start.1
  6.5 0.0 reduce-scatter.3.cloned.1.call-start
  6.5 1.6 %fusion.13 = (bf16[8,20,2048]{2,1,0:T(8,128)(2,1)S(1)}, bf16[8,20,2048]{2,1,0:T(8,128)(2,1)S(1)}) fusion(bf16[8,96,2048]{2,1,0:T(8,128)(2,1)} %refs_2_.1), kind=kLoop, calls=%fused_computation.33 | loop fusion | bytes 2621440 | tf_op jit(solution)/shard_map/slice | solution.py:175
  8.2 0.4 copy.20
  8.6 1.9 %collective-permute-start = (bf16[8,20,2048]{2,0,1:T(8,128)(2,1)S(1)}, bf16[8,20,2048]{2,0,1:T(8,128)(2,1)S(1)}, u32[]{:S(2)}, u32[]{:S(2)}) collective-permute-start(bf16[8,20,2048]{2,0,1:T(8,128)(2,1)S(1)} %copy.20), channel_id=1, source_target_pairs={{0,4},{4,8},{8,12},{12,16},{16,20},{20,24},{24,28},{28,32},{32,36}... | collective-permute-start | bytes 1966088 | tf_op jit(solution)/shard_map/ppermute | solution.py:172
  10.5 0.4 copy.21
  10.9 5.8 %collective-permute-start.1 = (bf16[8,20,2048]{2,0,1:T(8,128)(2,1)S(1)}, bf16[8,20,2048]{2,0,1:T(8,128)(2,1)S(1)}, u32[]{:S(2)}, u32[]{:S(2)}) collective-permute-start(bf16[8,20,2048]{2,0,1:T(8,128)(2,1)S(1)} %copy.21), channel_id=1, source_target_pairs={{4,0},{8,4},{12,8},{16,12},{20,16},{24,20},{28,24},{32,28},{36,32}... | collective-permute-start | bytes 1966088 | tf_op jit(solution)/shard_map/ppermute | solution.py:175
  17.3 0.0 copy-done.3
  17.3 0.1 dynamic_slice.6
  17.4 0.0 copy-done
  17.4 0.1 constant_dynamic-slice_fusion
  17.5 0.2 copy.13
  17.6 0.8 reshape.71.refs_1_
  18.4 0.1 iota_subtract_fusion
  18.5 0.0 copy-done.1
  18.5 5.2 %fusion = bf16[512,256,11]{1,2,0:T(8,128)(2,1)S(1)} fusion(s32[512,256]{1,0:T(8,128)S(1)} %iota_subtract_fusion, bf16[11,41]{1,0:T(8,128)(2,1)S(1)} %copy-done.1), kind=kOutput, calls=%fused_computation.1 | convolution fusion | flops 123600896 | bytes 3408774 | tf_op jit(solution)/shard_map/kt,tpx->kpx/dot_general | solution.py:42
  23.8 0.0 copy-start.2
  23.8 2.7 %copy.25 = bf16[512,256,11]{1,0,2:T(8,128)(2,1)} copy(bf16[512,256,11]{1,2,0:T(8,128)(2,1)S(1)} %fusion) | data formatting | bytes 5767168 | tf_op jit(solution)/shard_map/kt,tpx->kpx/dot_general | solution.py:42
  26.4 0.1 subtract_add_fusion
  26.5 0.0 copy-done.2
  26.5 0.9 fusion.6
  27.4 1.3 copy.16
  28.7 0.6 pad_add_fusion.refs_0_
  29.4 0.0 collective-permute-done
  29.4 1.2 copy.18.refs_3_
  30.6 0.0 collective-permute-done.1
  30.6 1.3 copy.19.refs_4_
  31.9 15.5 %coadd.1 = (f32[96,2048]{1,0:T(8,128)}, f32[96,2048]{1,0:T(8,128)}) custom-call(s32[17]{0:T(128)} %pad_add_fusion.refs_0_, f32[264]{0:T(512)} %reshape.71.refs_1_, bf16[8,96,2048]{2,1,0:T(8,128)(2,1)} %refs_2_.1, bf16[8,20,2048]{2,1,0:T(8,128)(2,1)} %copy.18.refs_3_, bf16[8,20,2048]{2,1,0:T(8,128)(2,1)} %copy.19.refs_4_, bf16[8,96,2048]{2,1,0:T(8,128)(2,1)} %refs_5_.1, ...), custom_call_target="tpu_custom_call" | custom-call | tf_op jit(solution)/shard_map/coadd/pallas_call | solution.py:137
  47.4 0.0 reduce-scatter.3.cloned.1.call-update
  47.4 0.0 reduce-scatter.5.cloned.1.call-start
  47.4 0.7 reduce-scatter.5.cloned.1.call-update
  48.1 65.7 %reduce-scatter.3.cloned.1.call-done = f32[96,512]{1,0:T(8,128)} async-done(((f32[96,2048]{1,0:T(8,128)}), f32[96,512]{1,0:T(8,128)}) %reduce-scatter.3.cloned.1.call-update) | async-done | bytes 196624 | tf_op jit(solution)/shard_map/reduce_scatter | solution.py:194
  113.9 24.6 %reduce-scatter.5.cloned.1.call-done = f32[96,512]{1,0:T(8,128)} async-done(((f32[96,2048]{1,0:T(8,128)}), f32[96,512]{1,0:T(8,128)}) %reduce-scatter.5.cloned.1.call-update) | async-done | bytes 196624 | tf_op jit(solution)/shard_map/reduce_scatter | solution.py:195
  138.5 1.7 %add_divide_fusion = f32[96,512]{1,0:T(8,128)} fusion(f32[96,512]{1,0:T(8,128)} %reduce-scatter.3.cloned.1.call-done, f32[96,512]{1,0:T(8,128)} %reduce-scatter.5.cloned.1.call-done), kind=kLoop, calls=%fused_computation.11 | loop fusion | flops 98304 | bytes 589824 | tf_op jit(solution)/shard_map/div | solution.py:196
  (3 shorter events, 0.0 us)
Async XLA Ops:
  6.5 10.9 %copy-start = (f32[32,11,3]{0,2,1:T(4,128)S(1)}, f32[32,11,3]{0,2,1:T(4,128)}, u32[]{:S(2)}) copy-start(f32[32,11,3]{0,2,1:T(4,128)} %param.11) | copy-start | bytes 12676
  6.5 10.8 %copy-start.3 = (s32[32]{0:T(128)S(1)}, s32[32]{0:T(128)}, u32[]{:S(2)}) copy-start(s32[32]{0:T(128)} %param.12) | copy-start | bytes 388
  6.5 12.0 %copy-start.1 = (bf16[11,41]{1,0:T(8,128)(2,1)S(1)}, bf16[11,41]{1,0:T(8,128)(2,1)}, u32[]{:S(2)}) copy-start(bf16[11,41]{1,0:T(8,128)(2,1)} %param.10) | copy-start | bytes 2710
  6.5 107.3 %reduce-scatter.3.cloned.1.call-start = ((), (), s32[]{:S(2)}) async-start(), calls=%async_computation.2 | async-start | bytes 983040 | tf_op jit(solution)/shard_map/reduce_scatter | solution.py:194
  8.6 20.8 %collective-permute-start = (bf16[8,20,2048]{2,0,1:T(8,128)(2,1)S(1)}, bf16[8,20,2048]{2,0,1:T(8,128)(2,1)S(1)}, u32[]{:S(2)}, u32[]{:S(2)}) collective-permute-start(bf16[8,20,2048]{2,0,1:T(8,128)(2,1)S(1)} %copy.20), channel_id=1, source_target_pairs={{0,4},{4,8},{8,12},{12,16},{16,20},{20,24},{24,28},{28,32},{32,36}... | collective-permute-start | bytes 1966088 | tf_op jit(solution)/shard_map/ppermute | solution.py:172
  10.9 19.8 %collective-permute-start.1 = (bf16[8,20,2048]{2,0,1:T(8,128)(2,1)S(1)}, bf16[8,20,2048]{2,0,1:T(8,128)(2,1)S(1)}, u32[]{:S(2)}, u32[]{:S(2)}) collective-permute-start(bf16[8,20,2048]{2,0,1:T(8,128)(2,1)S(1)} %copy.21), channel_id=1, source_target_pairs={{4,0},{8,4},{12,8},{16,12},{20,16},{24,20},{28,24},{32,28},{36,32}... | collective-permute-start | bytes 1966088 | tf_op jit(solution)/shard_map/ppermute | solution.py:175
  23.8 2.8 %copy-start.2 = (bf16[11,41]{1,0:T(8,128)(2,1)S(1)}, bf16[11,41]{1,0:T(8,128)(2,1)}, u32[]{:S(2)}) copy-start(bf16[11,41]{1,0:T(8,128)(2,1)} %param.9) | copy-start | bytes 2710
  47.4 91.1 %reduce-scatter.5.cloned.1.call-start = ((), (), s32[]{:S(2)}) async-start(), calls=%async_computation.3 | async-start | bytes 983040 | tf_op jit(solution)/shard_map/reduce_scatter | solution.py:195
Sparse Core Ops, SparseCore 0:
  47.5 66.3 reduce-scatter.2
  116.3 22.1 reduce-scatter.4

commit v2 on v1

--- a/solution.py
+++ b/solution.py
@@ -52,11 +52,12 @@
     inv_var,
     rows_ref,
     cols_ref,
-    num_ref,
-    den_ref,
+    own_ref,
+    send_ref,
     source,
     passed,
     matched,
+    num_ref,
     *,
     total_rows,
 ):
@@ -73,7 +74,6 @@
         source[...] = jnp.zeros_like(source)
         passed[...] = jnp.zeros_like(passed)
         num_ref[...] = jnp.zeros_like(num_ref)
-        den_ref[...] = jnp.zeros_like(den_ref)
 
     covered = scalars[1 + visit]
     shift = scalars[1 + visit_count + visit]
@@ -126,17 +126,84 @@
         inside = (col_ids[0:1] >= shift) & (col_ids[0:1] < shift + (col_count - DITHER))
         weight = inv_var[0].astype(jnp.float32) * inside.astype(jnp.float32)
         num_ref[...] += weight * matched[...]
-        den_ref[...] += weight
-
-
-def partial_sums(scalars, coeffs, images, top, bottom, inv_var, rows, cols, total_rows):
+
+    @pl.when(visit == visit_count - 1)
+    def _():
+        split_strips(scalars[1 + 2 * visit_count], num_ref, own_ref, send_ref)
+
+
+def split_strips(group, total, own_ref, send_ref):
+    groups = send_ref.shape[0] + 1
+    width = own_ref.shape[1]
+    for ahead in range(groups):
+        at = pl.multiple_of(lax.rem(group + ahead, groups) * width, width)
+        strip = total[:, pl.ds(at, width)]
+        if ahead == 0:
+            own_ref[...] = strip
+        else:
+            send_ref[ahead - 1] = strip.astype(jnp.bfloat16)
+
+
+def weight_kernel(scalars, inv_var, own_ref, send_ref, den_ref):
+    visit_count, row_count, col_count = inv_var.shape
+    col_ids = lax.broadcasted_iota(jnp.int32, (1, col_count), 1)
+    den_ref[...] = jnp.zeros_like(den_ref)
+
+    def step(visit, carry):
+        shift = scalars[1 + visit_count + visit]
+
+        @pl.when(scalars[1 + visit] > 0)
+        def _():
+            inside = (col_ids >= shift) & (col_ids < shift + (col_count - DITHER))
+            den_ref[...] += inv_var[visit].astype(jnp.float32) * inside.astype(jnp.float32)
+
+        return carry
+
+    lax.fori_loop(0, visit_count, step, 0)
+    split_strips(scalars[1 + 2 * visit_count], den_ref, own_ref, send_ref)
+
+
+def strip_shapes(row_count, col_count, groups):
+    width = col_count // groups
+    return (
+        jax.ShapeDtypeStruct((row_count, width), jnp.float32),
+        jax.ShapeDtypeStruct((groups - 1, row_count, width), jnp.bfloat16),
+    )
+
+
+def weight_sums(scalars, inv_var, groups):
+    visit_count, row_count, col_count = inv_var.shape
+    return pl.pallas_call(
+        weight_kernel,
+        out_shape=strip_shapes(row_count, col_count, groups),
+        in_specs=[
+            pl.BlockSpec(memory_space=pltpu.SMEM),
+            pl.BlockSpec(memory_space=pltpu.VMEM),
+        ],
+        out_specs=[pl.BlockSpec(memory_space=pltpu.VMEM)] * 2,
+        scratch_shapes=[pltpu.VMEM((row_count, col_count), jnp.float32)],
+        name="weights",
+    )(scalars, inv_var)
+
+
+def exchange(own, sends, axis):
+    groups = sends.shape[0] + 1
+    for ahead in range(1, groups):
+        got = lax.ppermute(
+            sends[ahead - 1], axis, [(i, (i + ahead) % groups) for i in range(groups)]
+        )
+        own = own + got.astype(jnp.float32)
+    return own
+
+
+def partial_sums(scalars, coeffs, images, top, bottom, inv_var, rows, cols, total_rows, groups):
     visit_count, row_count, col_count = images.shape
     half = top.shape[1]
-    plane = jax.ShapeDtypeStruct((row_count, col_count), jnp.float32)
+    shapes = strip_shapes(row_count, col_count, groups)
     whole = lambda shape: pl.BlockSpec(shape, lambda v, *_: (0,) * len(shape))
     return pl.pallas_call(
         lambda *refs: coadd_kernel(*refs, total_rows=total_rows),
-        out_shape=(plane, plane),
+        out_shape=shapes,
         grid_spec=pltpu.PrefetchScalarGridSpec(
             num_scalar_prefetch=2,
             grid=(visit_count,),
@@ -148,10 +215,11 @@
                 whole(rows.shape),
                 whole(cols.shape),
             ],
-            out_specs=[whole((row_count, col_count))] * 2,
+            out_specs=[whole(shape.shape) for shape in shapes],
             scratch_shapes=[
                 pltpu.VMEM((row_count + 64, col_count), jnp.bfloat16),
                 pltpu.VMEM((rows.shape[0], col_count + 2 * SIDE), jnp.bfloat16),
+                pltpu.VMEM((row_count, col_count), jnp.float32),
                 pltpu.VMEM((row_count, col_count), jnp.float32),
             ],
         ),
@@ -168,7 +236,8 @@
     sky = lax.axis_index("sky")
     tiles = lax.axis_size("sky")
     group = lax.axis_index("visit")
-    visits_all = visit_count * lax.axis_size("visit")
+    groups = lax.axis_size("visit")
+    visits_all = visit_count * groups
     top = lax.ppermute(
         images[:, row_count - half :], "sky", [(i, i + 1) for i in range(tiles - 1)]
     )
@@ -177,10 +246,12 @@
     covered = jnp.mod(order - sky * visits_all // tiles, visits_all) < depths[0]
     shifts = lax.dynamic_slice_in_dim(dithers, group * visit_count, visit_count, 0)
     scalars = jnp.concatenate(
-        [(sky * row_count)[None].astype(jnp.int32), covered.astype(jnp.int32), shifts]
-    )
+        [(sky * row_count)[None], covered.astype(jnp.int32), shifts, group[None]]
+    )
+    den_own, den_sends = weight_sums(scalars, inv_var, groups)
+    denominator = exchange(den_own, den_sends, "visit")
     coefs = lax.dynamic_slice_in_dim(coeffs, group * visit_count, visit_count, 0).reshape(-1)
-    numerator, denominator = partial_sums(
+    num_own, num_sends = partial_sums(
         scalars,
         coefs,
         images,
@@ -190,9 +261,9 @@
         row_table(row_taps, row_count),
         col_table(col_taps),
         row_count * tiles,
-    )
-    numerator = lax.psum_scatter(numerator, "visit", scatter_dimension=1, tiled=True)
-    denominator = lax.psum_scatter(denominator, "visit", scatter_dimension=1, tiled=True)
+        groups,
+    )
+    numerator = exchange(num_own, num_sends, "visit")
     return numerator / (1.0 + denominator)
 
 

time: 147 us -> 109 us (0.74)
  waiting for transfers between devices: 91.1 us -> 4.55 us
  Pallas kernels: 15.5 us -> 62.2 us
  between operations: 14.2 us -> 0.79 us
  starting transfers between devices: 7.72 us -> 16.7 us
  local copies, waits for them, and re-layouts: 9.92 us -> 14.9 us
    reduce_scatter x2 -> x0, waiting for transfers between devices: 90.4 us -> none  [the longest x1 65.7 us: local(): lax.psum_scatter(numerator, 'visit', scatter_dimension=1, tiled=True)]
    pallas_call x1, Pallas kernels: 15.5 us -> 58.5 us  [partial_sums(): pl.pallas_call(lambda *refs: coadd_kernel(*refs, total_rows=total_rows),...]
    ppermute x0 -> x6, starting transfers between devices: none -> 9.01 us  [exchange(): lax.ppermute(sends[ahead - 1], axis, [(i, (i + ahead) % groups) for i in...]
    ppermute x0 -> x6, waiting for transfers between devices: none -> 4.54 us  [exchange(): lax.ppermute(sends[ahead - 1], axis, [(i, (i + ahead) % groups) for i in...]
    pallas_call x0 -> x1, Pallas kernels: none -> 3.68 us  [weight_sums(): pl.pallas_call(weight_kernel, out_shape=strip_shapes(row_count, col_count...]
    squeeze x0 -> x2, local copies, waits for them, and re-layouts: none -> 2.71 us  [exchange(): sends[ahead - 1]]
    dot_general x1, local copies, waits for them, and re-layouts: 2.65 us -> 4.87 us  [col_table(): jnp.einsum('kt,tpx->kpx', col_taps, picks, preferred_element_type=jnp.flo...]
  transfers between devices with their start and end apart: 4 -> 8, of which waited for: 2 -> 2; matrix products, arithmetic and copies ran while one was open for 9% -> 19% of each run, Pallas kernels for 0% -> 57%
where the time goes in v2:
time: 109 us
  Pallas kernels  62.2 us (57%)
  starting transfers between devices  16.7 us (15%)
  local copies, waits for them, and re-layouts  14.9 us (14%)
  matrix products  7.5 us (7%)
  waiting for transfers between devices  4.55 us (4%)
  other arithmetic  2.66 us (2%)
    pallas_call x1, Pallas kernels, partial_sums(): pl.pallas_call(lambda *refs: coadd_kernel(*refs, total_rows=total_rows),...  58.5 us
    ppermute x6, starting transfers between devices, exchange(): lax.ppermute(sends[ahead - 1], axis, [(i, (i + ahead) % groups) for i in...  9.01 us
    dot_general x1, matrix products, col_table(): jnp.einsum('kt,tpx->kpx', col_taps, picks, preferred_element_type=jnp.flo...  6.65 us
    ppermute x1, starting transfers between devices, local(): lax.ppermute(images[:, :half], 'sky', [(i + 1, i) for i in range(tiles -...  5.75 us
    dot_general x1, local copies, waits for them, and re-layouts, col_table(): jnp.einsum('kt,tpx->kpx', col_taps, picks, preferred_element_type=jnp.flo...  4.87 us
    ppermute x6, waiting for transfers between devices, exchange(): lax.ppermute(sends[ahead - 1], axis, [(i, (i + ahead) % groups) for i in...  4.54 us
    pallas_call x1, Pallas kernels, weight_sums(): pl.pallas_call(weight_kernel, out_shape=strip_shapes(row_count, col_count...  3.68 us
    squeeze x2, local copies, waits for them, and re-layouts, exchange(): sends[ahead - 1]  2.71 us
  transfers between devices with their start and end apart: 8, of which 2 were waited for; matrix products, arithmetic and copies ran while one was open for 19% of the time, Pallas kernels for 57%

profile of v2, /device:TPU:24, one launch (start us, length us, event | category | flops | bytes accessed | tf_op | source)
XLA Modules:
  0.0 109.3 jit_solution(128790733982881649)
XLA Ops:
  0.0 0.0 copy-start
  0.0 0.0 copy-start.4
  0.0 1.6 %fusion.13 = (bf16[8,20,2048]{2,1,0:T(8,128)(2,1)S(1)}, bf16[8,20,2048]{2,1,0:T(8,128)(2,1)S(1)}) fusion(bf16[8,96,2048]{2,1,0:T(8,128)(2,1)} %refs_2_.1), kind=kLoop, calls=%fused_computation.39 | loop fusion | bytes 2621440 | tf_op jit(solution)/shard_map/slice | solution.py:244
  1.6 0.0 copy-start.2
  1.6 0.4 copy.20
  2.0 1.9 %collective-permute-start = (bf16[8,20,2048]{2,0,1:T(8,128)(2,1)S(1)}, bf16[8,20,2048]{2,0,1:T(8,128)(2,1)S(1)}, u32[]{:S(2)}, u32[]{:S(2)}) collective-permute-start(bf16[8,20,2048]{2,0,1:T(8,128)(2,1)S(1)} %copy.20), channel_id=1, source_target_pairs={{0,4},{4,8},{8,12},{12,16},{16,20},{20,24},{24,28},{28,32},{32,36}... | collective-permute-start | bytes 1966088 | tf_op jit(solution)/shard_map/ppermute | solution.py:241
  3.9 0.4 copy.21
  4.3 5.8 %collective-permute-start.1 = (bf16[8,20,2048]{2,0,1:T(8,128)(2,1)S(1)}, bf16[8,20,2048]{2,0,1:T(8,128)(2,1)S(1)}, u32[]{:S(2)}, u32[]{:S(2)}) collective-permute-start(bf16[8,20,2048]{2,0,1:T(8,128)(2,1)S(1)} %copy.21), channel_id=1, source_target_pairs={{4,0},{8,4},{12,8},{16,12},{20,16},{24,20},{28,24},{32,28},{36,32}... | collective-permute-start | bytes 1966088 | tf_op jit(solution)/shard_map/ppermute | solution.py:244
  10.8 0.0 copy-done.4
  10.8 0.1 dynamic_slice.6
  10.8 0.7 pad_add_fusion.refs_0_.scalars
  11.5 3.7 %weights.1 = (f32[96,512]{1,0:T(8,128)}, bf16[3,96,512]{2,1,0:T(8,128)(2,1)}) custom-call(s32[18]{0:T(128)} %pad_add_fusion.refs_0_.scalars, bf16[8,96,2048]{2,1,0:T(8,128)(2,1)} %inv_var.1), custom_call_target="tpu_custom_call" | custom-call | tf_op jit(solution)/shard_map/weights/pallas_call | solution.py:176
  15.2 1.7 %slice_bitcast_fusion.2 = (bf16[96,512]{1,0:T(8,128)(2,1)}, bf16[96,512]{1,0:T(8,128)(2,1)}, bf16[96,512]{1,0:T(8,128)(2,1)}) fusion(bf16[3,96,512]{2,1,0:T(8,128)(2,1)} %get-tuple-element.12), kind=kLoop, calls=%fused_computation.14 | loop fusion | bytes 589824 | tf_op jit(solution)/shard_map/squeeze | solution.py:193
  16.9 1.1 %collective-permute-start.5 = (bf16[96,512]{1,0:T(8,128)(2,1)}, bf16[96,512]{1,0:T(8,128)(2,1)S(1)}, u32[]{:S(2)}, u32[]{:S(2)}) collective-permute-start(bf16[96,512]{1,0:T(8,128)(2,1)} %get-tuple-element.18), channel_id=1, source_target_pairs={{0,1},{1,2},{2,3},{3,0},{4,5},{5,6},{6,7},{7,4},{8,9},{9,10},{10,1... | collective-permute-start | bytes 294920 | tf_op jit(solution)/shard_map/ppermute | solution.py:192
  18.0 4.4 %collective-permute-start.6 = (bf16[96,512]{1,0:T(8,128)(2,1)}, bf16[96,512]{1,0:T(8,128)(2,1)S(1)}, u32[]{:S(2)}, u32[]{:S(2)}) collective-permute-start(bf16[96,512]{1,0:T(8,128)(2,1)} %get-tuple-element.20), channel_id=1, source_target_pairs={{0,2},{1,3},{2,0},{3,1},{4,6},{5,7},{6,4},{7,5},{8,10},{9,11},{10,... | collective-permute-start | bytes 294920 | tf_op jit(solution)/shard_map/ppermute | solution.py:192
  22.4 0.2 collective-permute-start.7
  22.6 0.1 iota_subtract_fusion
  22.7 0.0 copy-done.2
  22.7 6.6 %fusion = bf16[512,256,11]{1,2,0:T(8,128)(2,1)} fusion(s32[512,256]{1,0:T(8,128)S(1)} %iota_subtract_fusion, bf16[11,41]{1,0:T(8,128)(2,1)S(1)} %copy-done.2), kind=kOutput, calls=%fused_computation.1 | convolution fusion | flops 123600896 | bytes 3408774 | tf_op jit(solution)/shard_map/kt,tpx->kpx/dot_general | solution.py:42
  29.4 0.0 copy-done
  29.4 0.0 copy-start.3
  29.4 0.1 constant_dynamic-slice_fusion
  29.5 0.2 copy.13
  29.6 0.8 reshape.71.refs_1_
  30.4 4.9 %copy.25 = bf16[512,256,11]{1,0,2:T(8,128)(2,1)} copy(bf16[512,256,11]{1,2,0:T(8,128)(2,1)} %fusion) | data formatting | bytes 5767168 | tf_op jit(solution)/shard_map/kt,tpx->kpx/dot_general | solution.py:42
  35.3 0.1 subtract_add_fusion
  35.3 0.0 copy-done.3
  35.4 0.9 fusion.6
  36.2 1.3 %copy.16 = bf16[11,96,160]{2,1,0:T(8,128)(2,1)} copy(bf16[11,96,160]{1,0,2:T(8,128)(2,1)S(1)} %fusion.6) | data formatting | bytes 675840 | tf_op jit(solution)/shard_map/convert_element_type | solution.py:27
  37.5 0.0 collective-permute-done
  37.5 1.3 %copy.18.refs_3_ = bf16[8,20,2048]{2,1,0:T(8,128)(2,1)} copy(bf16[8,20,2048]{2,0,1:T(8,128)(2,1)S(1)} %collective-permute-done) | data formatting | bytes 1310720 | tf_op jit(solution)/shard_map/ppermute | solution.py:241
  38.8 0.0 collective-permute-done.1
  38.8 1.3 %copy.19.refs_4_ = bf16[8,20,2048]{2,1,0:T(8,128)(2,1)} copy(bf16[8,20,2048]{2,0,1:T(8,128)(2,1)S(1)} %collective-permute-done.1) | data formatting | bytes 1310720 | tf_op jit(solution)/shard_map/ppermute | solution.py:244
  40.1 0.0 copy-start.1
  40.1 58.5 %coadd.1 = (f32[96,512]{1,0:T(8,128)}, bf16[3,96,512]{2,1,0:T(8,128)(2,1)}) custom-call(s32[18]{0:T(128)} %pad_add_fusion.refs_0_.scalars, f32[264]{0:T(512)} %reshape.71.refs_1_, bf16[8,96,2048]{2,1,0:T(8,128)(2,1)} %refs_2_.1, bf16[8,20,2048]{2,1,0:T(8,128)(2,1)} %copy.18.refs_3_, bf16[8,20,2048]{2,1,0:T(8,128)(2,1)} %copy.19.refs_4_, ...), custom_call_target="tpu_custom_call" | custom-call | tf_op jit(solution)/shard_map/coadd/pallas_call | solution.py:204
  98.6 1.0 slice_bitcast_fusion.5
  99.6 0.1 collective-permute-start.2
  99.7 1.8 %collective-permute-start.3 = (bf16[96,512]{1,0:T(8,128)(2,1)S(1)}, bf16[96,512]{1,0:T(8,128)(2,1)S(1)}, u32[]{:S(2)}, u32[]{:S(2)}) collective-permute-start(bf16[96,512]{1,0:T(8,128)(2,1)S(1)} %get-tuple-element.17), channel_id=1, source_target_pairs={{0,2},{1,3},{2,0},{3,1},{4,6},{5,7},{6,4},{7,5},{8,10},{9,11},{10,... | collective-permute-start | bytes 294920 | tf_op jit(solution)/shard_map/ppermute | solution.py:192
  101.5 0.0 collective-permute-done.5
  101.5 1.4 %collective-permute-start.4 = (bf16[96,512]{1,0:T(8,128)(2,1)S(1)}, bf16[96,512]{1,0:T(8,128)(2,1)S(1)}, u32[]{:S(2)}, u32[]{:S(2)}) collective-permute-start(bf16[96,512]{1,0:T(8,128)(2,1)S(1)} %get-tuple-element.16), channel_id=1, source_target_pairs={{0,3},{1,0},{2,1},{3,2},{4,7},{5,4},{6,5},{7,6},{8,11},{9,8},{10,9... | collective-permute-start | bytes 294920 | tf_op jit(solution)/shard_map/ppermute | solution.py:192
  102.9 0.0 collective-permute-done.6
  102.9 0.0 collective-permute-done.7
  102.9 3.6 %collective-permute-done.2 = bf16[96,512]{1,0:T(8,128)(2,1)S(1)} collective-permute-done((bf16[96,512]{1,0:T(8,128)(2,1)S(1)}, bf16[96,512]{1,0:T(8,128)(2,1)S(1)}, u32[]{:S(2)}, u32[]{:S(2)}) %collective-permute-start.2) | collective-permute-done | bytes 98336 | tf_op jit(solution)/shard_map/ppermute | solution.py:192
  106.6 0.0 collective-permute-done.3
  106.6 0.9 collective-permute-done.4
  107.5 0.0 copy-done.1
  107.5 1.8 %add_divide_fusion = f32[96,512]{1,0:T(8,128)} fusion(bf16[96,512]{1,0:T(8,128)(2,1)} %collective-permute-done.7, bf16[96,512]{1,0:T(8,128)(2,1)S(1)} %collective-permute-done.6, f32[96,512]{1,0:T(8,128)S(1)} %copy-done.1, bf16[96,512]{1,0:T(8,128)(2,1)S(1)} %collective-permute-done.5, bf16[96,512]{1,0:T(8,128)(2,1)S(1)} %collective-permute-done.4, ...), kind=kLoop, calls=%fused_computation.11 | loop fusion | flops 688128 | bytes 1179648 | tf_op jit(solution)/shard_map/div | solution.py:267
  (3 shorter events, 0.0 us)
Async XLA Ops:
  0.0 29.4 %copy-start = (f32[32,11,3]{0,2,1:T(4,128)S(1)}, f32[32,11,3]{0,2,1:T(4,128)}, u32[]{:S(2)}) copy-start(f32[32,11,3]{0,2,1:T(4,128)} %param.11) | copy-start | bytes 12676
  0.0 10.8 %copy-start.4 = (s32[32]{0:T(128)S(1)}, s32[32]{0:T(128)}, u32[]{:S(2)}) copy-start(s32[32]{0:T(128)} %param.12) | copy-start | bytes 388
  1.6 21.1 %copy-start.2 = (bf16[11,41]{1,0:T(8,128)(2,1)S(1)}, bf16[11,41]{1,0:T(8,128)(2,1)}, u32[]{:S(2)}) copy-start(bf16[11,41]{1,0:T(8,128)(2,1)} %param.10) | copy-start | bytes 2710
  2.0 35.5 %collective-permute-start = (bf16[8,20,2048]{2,0,1:T(8,128)(2,1)S(1)}, bf16[8,20,2048]{2,0,1:T(8,128)(2,1)S(1)}, u32[]{:S(2)}, u32[]{:S(2)}) collective-permute-start(bf16[8,20,2048]{2,0,1:T(8,128)(2,1)S(1)} %copy.20), channel_id=1, source_target_pairs={{0,4},{4,8},{8,12},{12,16},{16,20},{20,24},{24,28},{28,32},{32,36}... | collective-permute-start | bytes 1966088 | tf_op jit(solution)/shard_map/ppermute | solution.py:241
  4.3 34.5 %collective-permute-start.1 = (bf16[8,20,2048]{2,0,1:T(8,128)(2,1)S(1)}, bf16[8,20,2048]{2,0,1:T(8,128)(2,1)S(1)}, u32[]{:S(2)}, u32[]{:S(2)}) collective-permute-start(bf16[8,20,2048]{2,0,1:T(8,128)(2,1)S(1)} %copy.21), channel_id=1, source_target_pairs={{4,0},{8,4},{12,8},{16,12},{20,16},{24,20},{28,24},{32,28},{36,32}... | collective-permute-start | bytes 1966088 | tf_op jit(solution)/shard_map/ppermute | solution.py:244
  16.9 84.6 %collective-permute-start.5 = (bf16[96,512]{1,0:T(8,128)(2,1)}, bf16[96,512]{1,0:T(8,128)(2,1)S(1)}, u32[]{:S(2)}, u32[]{:S(2)}) collective-permute-start(bf16[96,512]{1,0:T(8,128)(2,1)} %get-tuple-element.18), channel_id=1, source_target_pairs={{0,1},{1,2},{2,3},{3,0},{4,5},{5,6},{6,7},{7,4},{8,9},{9,10},{10,1... | collective-permute-start | bytes 294920 | tf_op jit(solution)/shard_map/ppermute | solution.py:192
  18.0 84.9 %collective-permute-start.6 = (bf16[96,512]{1,0:T(8,128)(2,1)}, bf16[96,512]{1,0:T(8,128)(2,1)S(1)}, u32[]{:S(2)}, u32[]{:S(2)}) collective-permute-start(bf16[96,512]{1,0:T(8,128)(2,1)} %get-tuple-element.20), channel_id=1, source_target_pairs={{0,2},{1,3},{2,0},{3,1},{4,6},{5,7},{6,4},{7,5},{8,10},{9,11},{10,... | collective-permute-start | bytes 294920 | tf_op jit(solution)/shard_map/ppermute | solution.py:192
  22.4 80.6 %collective-permute-start.7 = (bf16[96,512]{1,0:T(8,128)(2,1)}, bf16[96,512]{1,0:T(8,128)(2,1)}, u32[]{:S(2)}, u32[]{:S(2)}) collective-permute-start(bf16[96,512]{1,0:T(8,128)(2,1)} %get-tuple-element.19), channel_id=1, source_target_pairs={{0,3},{1,0},{2,1},{3,2},{4,7},{5,4},{6,5},{7,6},{8,11},{9,8},{10,9... | collective-permute-start | bytes 294920 | tf_op jit(solution)/shard_map/ppermute | solution.py:192
  29.4 6.0 %copy-start.3 = (bf16[11,41]{1,0:T(8,128)(2,1)S(1)}, bf16[11,41]{1,0:T(8,128)(2,1)}, u32[]{:S(2)}) copy-start(bf16[11,41]{1,0:T(8,128)(2,1)} %param.9) | copy-start | bytes 2710
  40.1 67.4 %copy-start.1 = (f32[96,512]{1,0:T(8,128)S(1)}, f32[96,512]{1,0:T(8,128)}, u32[]{:S(2)}) copy-start(f32[96,512]{1,0:T(8,128)} %get-tuple-element.11) | copy-start | bytes 589828
  99.6 6.9 %collective-permute-start.2 = (bf16[96,512]{1,0:T(8,128)(2,1)S(1)}, bf16[96,512]{1,0:T(8,128)(2,1)S(1)}, u32[]{:S(2)}, u32[]{:S(2)}) collective-permute-start(bf16[96,512]{1,0:T(8,128)(2,1)S(1)} %get-tuple-element.15), channel_id=1, source_target_pairs={{0,1},{1,2},{2,3},{3,0},{4,5},{5,6},{6,7},{7,4},{8,9},{9,10},{10,1... | collective-permute-start | bytes 294920 | tf_op jit(solution)/shard_map/ppermute | solution.py:192
  99.7 6.9 %collective-permute-start.3 = (bf16[96,512]{1,0:T(8,128)(2,1)S(1)}, bf16[96,512]{1,0:T(8,128)(2,1)S(1)}, u32[]{:S(2)}, u32[]{:S(2)}) collective-permute-start(bf16[96,512]{1,0:T(8,128)(2,1)S(1)} %get-tuple-element.17), channel_id=1, source_target_pairs={{0,2},{1,3},{2,0},{3,1},{4,6},{5,7},{6,4},{7,5},{8,10},{9,11},{10,... | collective-permute-start | bytes 294920 | tf_op jit(solution)/shard_map/ppermute | solution.py:192
  101.5 5.9 %collective-permute-start.4 = (bf16[96,512]{1,0:T(8,128)(2,1)S(1)}, bf16[96,512]{1,0:T(8,128)(2,1)S(1)}, u32[]{:S(2)}, u32[]{:S(2)}) collective-permute-start(bf16[96,512]{1,0:T(8,128)(2,1)S(1)} %get-tuple-element.16), channel_id=1, source_target_pairs={{0,3},{1,0},{2,1},{3,2},{4,7},{5,4},{6,5},{7,6},{8,11},{9,8},{10,9... | collective-permute-start | bytes 294920 | tf_op jit(solution)/shard_map/ppermute | solution.py:192
